TPU v7x, 512 devices: a whole 4x4x16 slice. The times are simulated.
512 devices in a mesh: band: 128 (over z_lo, y, x, core), head: 4 (over z_hi).
Axes of the slice: x: 4, y: 4, z: 16 (z_hi: 4, z_lo: 4; z = z_hi * 4 + z_lo), core: 2. Of those that a mesh axis runs over, the one named last changes fastest.
Arguments:
- queries: bfloat16 [256, 131072], P('head', 'band'), may hold values from -76 to 76
- keys: bfloat16 [256, 131072], P('head', 'band'), may hold values from -6 to 6
- values: bfloat16 [256, 131072], P('head', 'band'), may hold values from -6 to 6
- grad_out: bfloat16 [256, 131072], P('head', 'band'), may hold values from -6 to 6
- w_out: bfloat16 [256, 256], P('head'), may hold values from -0.375 to 0.375
- key_lists: int32 [1024, 8], P('band'), may hold values from 0 to 1023, as said below
- key_counts: int32 [1024], P('band'), may hold values from 2 to 8, as said below
Outputs:
- grad_queries: bfloat16 [256, 131072], P('head', 'band')
- grad_keys: bfloat16 [256, 131072], P('head', 'band')
- grad_values: bfloat16 [256, 131072], P('head', 'band')
- grad_w_out: float32 [256, 256], P('head')
Inputs may be any that keep to these rules, and one draw needn't show every extreme that they name: `key_lists`: row b holds 8 different blocks; the first is b itself and every entry lies within 8 blocks of b. `key_counts`: the number of leading entries of the row of key_lists that are used.
All inputs are finite; a program needn't handle non-finite values.
Results may differ from a plain program's by a relative error of at most 0.0058.
Values may be sent and summed in bfloat16 or wider, within the bound.
A program may use at most 64 MiB of HBM per device.

v0:
```python
import jax
import jax.numpy as jnp
from jax import lax
from jax.sharding import PartitionSpec as P

HEAD_DIM = 32
BLOCK = 128
REACH = 4
MAX_KEYS = 8


def with_halo(block, sides, width):
    for axis, dim in sides:
        count = lax.axis_size(axis)
        forward = [(i, i + 1) for i in range(count - 1)]
        backward = [(target, source) for source, target in forward]
        low = lax.ppermute(
            lax.slice_in_dim(block, block.shape[dim] - width, None, axis=dim), axis, forward
        )
        high = lax.ppermute(lax.slice_in_dim(block, 0, width, axis=dim), axis, backward)
        block = jnp.concatenate([low, block, high], axis=dim)
    return block


def shifted(value, axis, steps):
    count = lax.axis_size(axis)
    initial, last = (max(0, -steps), min(count, count - steps))
    return lax.ppermute(value, axis, [(source, source + steps) for source in range(initial, last)])


def block_grads(query_blk, grad_blk, slots, usable, key_ext, value_ext, bias_ext):
    count = slots.shape[0]
    span = count * BLOCK
    chans = query_blk.shape[0]
    heads_here = chans // HEAD_DIM
    scale = HEAD_DIM ** (-0.5)
    picked_k = key_ext[:, slots].reshape(heads_here, HEAD_DIM, span)
    picked_v = value_ext[:, slots].reshape(heads_here, HEAD_DIM, span)
    key_bias = bias_ext[slots].reshape(span)
    live_keys = jnp.repeat(usable, BLOCK)
    query_h = query_blk.reshape(heads_here, HEAD_DIM, BLOCK)
    grad_h = grad_blk.reshape(heads_here, HEAD_DIM, BLOCK)
    scores = (
        jnp.einsum("hdq,hdk->hqk", query_h, picked_k, preferred_element_type=jnp.float32) * scale
        + key_bias
    )
    scores = jnp.where(live_keys, scores, -jnp.inf)
    peak = jnp.max(scores, axis=-1)
    log_total = peak + jnp.log(jnp.sum(jnp.exp(scores - peak[..., None]), axis=-1))
    probs = jnp.exp(scores - log_total[..., None])
    probs_low = probs.astype(jnp.bfloat16)
    dprobs = jnp.einsum("hdq,hdk->hqk", grad_h, picked_v, preferred_element_type=jnp.float32)
    spread = jnp.sum(probs * dprobs, axis=-1)
    dscores = (probs * (dprobs - spread[..., None]) * scale).astype(jnp.bfloat16)
    dquery = jnp.einsum(
        "hqk,hdk->hdq", dscores, picked_k, preferred_element_type=jnp.float32
    ).reshape(chans, BLOCK)
    dkey = jnp.einsum("hqk,hdq->hdk", dscores, query_h, preferred_element_type=jnp.float32).reshape(
        chans, count, BLOCK
    )
    dvalue = jnp.einsum(
        "hqk,hdq->hdk", probs_low, grad_h, preferred_element_type=jnp.float32
    ).reshape(chans, count, BLOCK)
    attended = jnp.einsum(
        "hqk,hdk->hdq", probs_low, picked_v, preferred_element_type=jnp.float32
    ).reshape(chans, BLOCK)
    return (dquery, dkey, dvalue, attended, log_total, spread)


def band_bias(first_block, ext_blocks, total_tokens):
    positions = first_block * BLOCK + jnp.arange(ext_blocks * BLOCK, dtype=jnp.int32)
    positions = jnp.clip(positions, 0, total_tokens - 1).astype(jnp.float32)
    return jnp.log(jnp.sin(jnp.pi * (positions + 0.5) / total_tokens)).reshape(ext_blocks, BLOCK)


def run_blocks(query_blocks, grad_blocks, slot_rows, use_rows, key_ext, value_ext, bias_ext):
    chans = query_blocks.shape[0]
    nblocks = query_blocks.shape[1]
    heads_here = chans // HEAD_DIM
    ext_blocks = key_ext.shape[1]
    zeros = jnp.zeros((chans, ext_blocks, BLOCK), jnp.float32)
    start = (
        zeros,
        zeros,
        jnp.zeros((chans, nblocks, BLOCK), jnp.bfloat16),
        jnp.zeros((chans, nblocks, BLOCK), jnp.bfloat16),
        jnp.zeros((nblocks, heads_here, BLOCK), jnp.float32),
        jnp.zeros((nblocks, heads_here, BLOCK), jnp.float32),
    )

    def run_width(index, carry):
        acc_k, acc_v, dq_all, att_all, lse_all, spread_all = carry
        query_blk = lax.dynamic_index_in_dim(query_blocks, index, 1, keepdims=False)
        grad_blk = lax.dynamic_index_in_dim(grad_blocks, index, 1, keepdims=False)
        slots = slot_rows[index]
        dquery, dkey, dvalue, attended, log_total, spread = block_grads(
            query_blk, grad_blk, slots, use_rows[index], key_ext, value_ext, bias_ext
        )
        acc_k = acc_k.at[:, slots].add(dkey)
        acc_v = acc_v.at[:, slots].add(dvalue)
        dq_all = dq_all.at[:, index].set(dquery.astype(jnp.bfloat16))
        att_all = att_all.at[:, index].set(attended.astype(jnp.bfloat16))
        lse_all = lse_all.at[index].set(log_total)
        spread_all = spread_all.at[index].set(spread)
        return (acc_k, acc_v, dq_all, att_all, lse_all, spread_all)

    def block_step(index, carry):
        return run_width(index, carry)

    return lax.fori_loop(0, nblocks, block_step, start)


def shards(queries, keys, values, grad_out, w_out, key_lists, key_counts):
    chans = queries.shape[0]
    blocks = queries.shape[1] // BLOCK
    rim_blocks = 2 * REACH
    ext_blocks = blocks + 2 * rim_blocks
    band_index = lax.axis_index("band")
    band_count = lax.axis_size("band")
    total_tokens = blocks * BLOCK * band_count
    full_grad = lax.all_gather(grad_out, "head", axis=0, tiled=True)
    grad_att = jnp.einsum("cd,dt->ct", w_out, full_grad, preferred_element_type=jnp.float32).astype(
        jnp.bfloat16
    )
    key_pairs = jnp.stack(
        [keys.reshape(chans, blocks, BLOCK), values.reshape(chans, blocks, BLOCK)]
    )
    pair_ext = with_halo(key_pairs, (("band", 2),), rim_blocks)
    key_ext = pair_ext[0]
    value_ext = pair_ext[1]
    first_block = band_index * blocks - rim_blocks
    bias_ext = band_bias(first_block, ext_blocks, total_tokens)
    slot_ids = jnp.arange(MAX_KEYS, dtype=jnp.int32)
    masked = jnp.where(slot_ids[None, :] < key_counts[:, None], key_lists, -1)
    usable = masked >= 0
    local_slots = jnp.clip(masked - first_block, 0, ext_blocks - 1)
    query_blocks = queries.reshape(chans, blocks, BLOCK)
    grad_blocks = grad_att.reshape(chans, blocks, BLOCK)
    acc_k, acc_v, dq_all, att_all, lse_all, spread_all = run_blocks(
        query_blocks, grad_blocks, local_slots, usable, key_ext, value_ext, bias_ext
    )
    lower_part = jnp.stack([acc_k[:, :rim_blocks], acc_v[:, :rim_blocks]])
    upper_part = jnp.stack([acc_k[:, rim_blocks + blocks :], acc_v[:, rim_blocks + blocks :]])
    from_above = shifted(lower_part.astype(jnp.bfloat16), "band", -1).astype(lower_part.dtype)
    from_below = shifted(upper_part.astype(jnp.bfloat16), "band", 1).astype(upper_part.dtype)
    owned = jnp.stack(
        [acc_k[:, rim_blocks : rim_blocks + blocks], acc_v[:, rim_blocks : rim_blocks + blocks]]
    )
    owned = owned.at[:, :, :rim_blocks].add(from_below)
    owned = owned.at[:, :, blocks - rim_blocks :].add(from_above)
    grad_queries = dq_all.reshape(chans, blocks * BLOCK)
    grad_keys = owned[0].reshape(chans, blocks * BLOCK).astype(jnp.bfloat16)
    grad_values = owned[1].reshape(chans, blocks * BLOCK).astype(jnp.bfloat16)
    attended = att_all.reshape(chans, blocks * BLOCK)
    partial_w = jnp.einsum("ct,dt->cd", attended, full_grad, preferred_element_type=jnp.float32)
    grad_w_out = lax.psum(partial_w, "band")
    return (grad_queries, grad_keys, grad_values, grad_w_out)


def solution(mesh):
    in_specs = (
        P("head", "band"),
        P("head", "band"),
        P("head", "band"),
        P("head", "band"),
        P("head", None),
        P("band", None),
        P("band"),
    )
    out_specs = (P("head", "band"), P("head", "band"), P("head", "band"), P("head", None))
    return jax.shard_map(shards, mesh=mesh, in_specs=in_specs, out_specs=out_specs, check_vma=False)
```

profile of v0, /device:TPU:128, one launch (start us, length us, event | category | flops | bytes accessed | tf_op | source)
XLA Modules:
  0.0 1363.9 jit_solution(3524123765928324000)
XLA Ops:
  10.5 3.0 collective-permute-start
  14.9 28.8 %all_gather.3 = bf16[256,1024]{1,0:T(8,128)(2,1)S(1)} all-gather(bf16[64,1024]{1,0:T(8,128)(2,1)S(1)} %copy-done.10), channel_id=1, replica_groups=mesh['band'=128,'head'=4] {'head'}, dimensions={0}, use_global_device_ids=true | all-gather | bytes 655360 | tf_op jit(solution)/shard_map/all_gather | solution.py:121
  48.4 139.9 %while.26 = (s32[]{:T(128)}, f32[64,24,128]{2,0,1:T(8,128)}, f32[64,24,128]{2,0,1:T(8,128)S(1)}, bf16[64,8,128]{2,0,1:T(8,128)(2,1)S(1)}, bf16[64,8,128]{2,0,1:T...) while((s32[]{:T(128)}, f32[64,24,128]{2,0,1:T(8,128)}, ...), condition=%wide.region_7.8_spmd.clone, body=%wide.region_0.7_spmd.clone.sunk | while | flops 107143464 | bytes 23508944 | solution.py:110
  60.1 1.8 fusion.90
  62.0 2.0 constant_dynamic-update-slice_fusion.3
  70.1 1.6 gather_fusion.2
  77.5 1.8 fusion.90
  79.5 2.0 constant_dynamic-update-slice_fusion.3
  95.0 1.8 fusion.90
  97.0 2.0 constant_dynamic-update-slice_fusion.3
  112.5 1.8 fusion.90
  114.5 2.0 constant_dynamic-update-slice_fusion.3
  122.5 1.6 gather_fusion.2
  130.0 1.8 fusion.90
  131.9 2.0 constant_dynamic-update-slice_fusion.3
  147.5 1.8 fusion.90
  149.4 2.0 constant_dynamic-update-slice_fusion.3
  164.9 1.8 fusion.90
  166.9 2.0 constant_dynamic-update-slice_fusion.3
  182.4 1.8 fusion.90
  184.4 2.0 constant_dynamic-update-slice_fusion.3
  188.2 2.1 fusion.34
  191.9 3.0 collective-permute-start.2
  197.8 1157.8 %all-reduce.2.cloned.1.call-done = f32[64,256]{1,0:T(8,128)} async-done(((f32[64,256]{1,0:T(8,128)}), f32[64,256]{1,0:T(8,128)}) %all-reduce.2.cloned.1.call-update) | async-done | bytes 65552 | tf_op jit(solution)/shard_map/psum | solution.py:156
  (419 shorter events, 119.1 us)
Async XLA Ops:
  7.2 36.8 %copy-start = (bf16[64,1024]{1,0:T(8,128)(2,1)S(1)}, bf16[64,1024]{1,0:T(8,128)(2,1)}, u32[]{:S(2)}) copy-start(bf16[64,1024]{1,0:T(8,128)(2,1)} %param.21) | copy-start | bytes 393220
  7.2 6.4 copy-start.15
  7.2 6.4 copy-start.14
  7.2 7.7 copy-start.10
  7.2 36.5 %copy-start.13 = (bf16[64,256]{1,0:T(8,128)(2,1)S(1)}, bf16[64,256]{1,0:T(8,128)(2,1)}, u32[]{:S(2)}) copy-start(bf16[64,256]{1,0:T(8,128)(2,1)} %param.25) | copy-start | bytes 98308
  7.2 1348.3 %all-reduce.2.cloned.1.call-start = ((), (), s32[]{:S(2)}) async-start(), calls=%async_computation | async-start | bytes 131072 | tf_op jit(solution)/shard_map/psum | solution.py:156
  9.2 35.4 %collective-permute-start.1 = (bf16[2,64,8,128]{3,2,1,0:T(8,128)(2,1)S(1)}, bf16[2,64,8,128]{3,2,1,0:T(8,128)(2,1)S(1)}, u32[]{:S(2)}, u32[]{:S(2)}) collective-permute-start(bf16[2,64,8,128]{3,2,1,0:T(8,128)(2,1)S(1)} %bitcast_dynamic-update-slice_fusion), channel_id=1, source_target_pairs={{4,0},{8,4},{12,8},{16,12},{20,16},{24,20},{28,24},{32,28},{36,32}... | collective-permute-start | bytes 786440 | tf_op jit(solution)/shard_map/ppermute | solution.py:20
  10.5 34.1 %collective-permute-start = (bf16[2,64,8,128]{3,2,1,0:T(8,128)(2,1)S(1)}, bf16[2,64,8,128]{3,2,1,0:T(8,128)(2,1)S(1)}, u32[]{:S(2)}, u32[]{:S(2)}) collective-permute-start(bf16[2,64,8,128]{3,2,1,0:T(8,128)(2,1)S(1)} %bitcast_dynamic-update-slice_fusion), channel_id=1, source_target_pairs={{0,4},{4,8},{8,12},{12,16},{16,20},{20,24},{24,28},{28,32},{32,36}... | collective-permute-start | bytes 786440 | tf_op jit(solution)/shard_map/ppermute | solution.py:17
  50.4 7.3 copy-start.11
  65.8 5.8 copy-start.7
  67.9 7.3 copy-start.11
  83.3 5.8 copy-start.7
  85.4 7.3 copy-start.11
  100.8 5.8 copy-start.7
  102.9 7.3 copy-start.11
  118.3 5.8 copy-start.7
  120.4 7.3 copy-start.11
  135.8 5.8 copy-start.7
  137.8 7.3 copy-start.11
  153.3 5.8 copy-start.7
  155.3 7.3 copy-start.11
  172.8 7.3 copy-start.11
  190.6 5.1 collective-permute-start.3
  191.9 4.2 collective-permute-start.2
  (60 other events, 159.7 us)
Sparse Core Ops, SparseCore 0:
  190.5 1165.0 all-reduce.1
where the time goes:
time: 1370 us; the launch traced here: 1360 us
  waiting for transfers between devices  1160 us (85%)
  local copies, waits for them, and re-layouts  63.2 us (5%)
  other arithmetic  51.8 us (4%)
  matrix products  37.2 us (3%)
  blocking collectives  28.8 us (2%)
  between operations  14.3 us (1%)
    psum x1, waiting for transfers between devices, shards(): grad_w_out = lax.psum(partial_w, 'band')  1160 us
    all_gather x1, blocking collectives, shards(): full_grad = lax.all_gather(grad_out, 'head', axis=0, tiled=True)  28.8 us
  transfers between devices with their start and end apart: 5, of which 2 were waited for; matrix products, arithmetic and copies ran while one was open for 0% of the time, Pallas kernels for 0%

commit v1 on v0

--- a/solution.py
+++ b/solution.py
@@ -2,6 +2,7 @@
 import jax.numpy as jnp
 from jax import lax
 from jax.sharding import PartitionSpec as P
+from jax.lax import all_gather
 
 HEAD_DIM = 32
 BLOCK = 128
@@ -153,7 +154,8 @@
     grad_values = owned[1].reshape(chans, blocks * BLOCK).astype(jnp.bfloat16)
     attended = att_all.reshape(chans, blocks * BLOCK)
     partial_w = jnp.einsum("ct,dt->cd", attended, full_grad, preferred_element_type=jnp.float32)
-    grad_w_out = lax.psum(partial_w, "band")
+    work_now = all_gather(partial_w, "band")
+    grad_w_out = jnp.sum(work_now, axis=0)
     return (grad_queries, grad_keys, grad_values, grad_w_out)
 
 

time: 1370 us -> 454 us (0.33)
  the two profiles are of different devices: /device:TPU:128 before, /device:TPU:1 now
where the time goes in v1:
time: 454 us; the launch traced here: 449 us
  waiting for transfers between devices  198 us (44%)
  other arithmetic  76.1 us (17%)
  local copies, waits for them, and re-layouts  62.2 us (14%)
  matrix products  53 us (12%)
  blocking collectives  27.7 us (6%)
  starting transfers between devices  17.5 us (4%)
  between operations  14.2 us (3%)
    all_gather x1, waiting for transfers between devices, shards(): work_now = all_gather(partial_w, 'band')  196 us
    all_gather x1, blocking collectives, shards(): full_grad = lax.all_gather(grad_out, 'head', axis=0, tiled=True)  27.7 us
    scatter-add x8, other arithmetic, run_width(): acc_v = acc_v.at[:, slots].add(dvalue)  19 us
    scatter x8, other arithmetic, run_width(): att_all = att_all.at[:, index].set(attended.astype(jnp.bfloat16))  16.1 us
    dot_general x8, matrix products, block_grads(): jnp.einsum('hqk,hdq->hdk', dscores, query_h, preferred_element_type=jnp.f...  14.6 us
    dot_general x8, matrix products, block_grads(): jnp.einsum('hqk,hdk->hdq', dscores, picked_k, preferred_element_type=jnp....  13.6 us
    gather x16, local copies, waits for them, and re-layouts, block_grads(): picked_k = key_ext[:, slots].reshape(heads_here, HEAD_DIM, span)  13.3 us
    gather x16, local copies, waits for them, and re-layouts, block_grads(): picked_v = value_ext[:, slots].reshape(heads_here, HEAD_DIM, span)  13.3 us
  transfers between devices with their start and end apart: 5, of which 3 were waited for; matrix products, arithmetic and copies ran while one was open for 2% of the time, Pallas kernels for 0%

profile of v1, /device:TPU:1, one launch (start us, length us, event | category | flops | bytes accessed | tf_op | source)
XLA Modules:
  0.0 449.3 jit_solution(14129657560128938277)
XLA Ops:
  9.1 8.7 %collective-permute-start.1 = (bf16[2,64,8,128]{3,2,1,0:T(8,128)(2,1)S(1)}, bf16[2,64,8,128]{3,2,1,0:T(8,128)(2,1)S(1)}, u32[]{:S(2)}, u32[]{:S(2)}) collective-permute-start(bf16[2,64,8,128]{3,2,1,0:T(8,128)(2,1)S(1)} %bitcast_dynamic-update-slice_fusion), channel_id=1, source_target_pairs={{4,0},{8,4},{12,8},{16,12},{20,16},{24,20},{28,24},{32,28},{36,32}... | collective-permute-start | bytes 786440 | tf_op jit(solution)/shard_map/ppermute | solution.py:21
  22.5 27.7 %all_gather.9 = bf16[256,1024]{1,0:T(8,128)(2,1)S(1)} all-gather(bf16[64,1024]{1,0:T(8,128)(2,1)} %param.24), channel_id=1, replica_groups=mesh['band'=128,'head'=4] {'head'}, dimensions={0}, use_global_device_ids=true | all-gather | bytes 655360 | tf_op jit(solution)/shard_map/all_gather | solution.py:122
  56.2 170.6 %while.26 = (s32[]{:T(128)}, f32[64,24,128]{2,0,1:T(8,128)S(1)}, f32[64,24,128]{2,0,1:T(8,128)}, bf16[64,8,128]{2,0,1:T(8,128)(2,1)}, bf16[64,8,128]{2,0,1:T(8,1...) while((s32[]{:T(128)}, f32[64,24,128]{2,0,1:T(8,128)S(1)}, ...), condition=%wide.region_7.8_spmd.clone, body=%wide.region_0.7_spmd.clone.sunk | while | flops 107143464 | bytes 16098958 | solution.py:111
  69.0 2.4 scatter_fusion.1
  75.5 2.0 constant_dynamic-update-slice_fusion.3
  90.3 2.4 scatter_fusion.1
  96.8 2.0 constant_dynamic-update-slice_fusion.3
  111.6 2.4 scatter_fusion.1
  118.1 2.0 constant_dynamic-update-slice_fusion.3
  133.0 2.4 scatter_fusion.1
  139.5 2.0 constant_dynamic-update-slice_fusion.3
  154.3 2.4 scatter_fusion.1
  160.8 2.0 constant_dynamic-update-slice_fusion.3
  175.6 2.4 scatter_fusion.1
  182.1 2.0 constant_dynamic-update-slice_fusion.3
  196.9 2.4 scatter_fusion.1
  203.4 2.0 constant_dynamic-update-slice_fusion.3
  218.2 2.4 scatter_fusion.1
  224.7 2.0 constant_dynamic-update-slice_fusion.3
  226.7 2.0 fusion.34
  230.1 4.1 collective-permute-start.3
  234.3 2.7 collective-permute-start.2
  242.0 196.0 %all-gather.3.cloned.1.call-done = f32[8192,256]{1,0:T(8,128)} async-done(((f32[64,256]{1,0:T(8,128)}), f32[8192,256]{1,0:T(8,128)}) %all-gather.3.cloned.1.call-update) | async-done | bytes 8388624 | tf_op jit(solution)/shard_map/all_gather | solution.py:157
  438.0 4.5 reduce_sum.35
  (301 shorter events, 153.2 us)
Async XLA Ops:
  7.2 43.9 %copy-start = (bf16[64,1024]{1,0:T(8,128)(2,1)S(1)}, bf16[64,1024]{1,0:T(8,128)(2,1)}, u32[]{:S(2)}) copy-start(bf16[64,1024]{1,0:T(8,128)(2,1)} %param.21) | copy-start | bytes 393220
  7.2 43.0 %copy-start.5 = (bf16[64,256]{1,0:T(8,128)(2,1)S(1)}, bf16[64,256]{1,0:T(8,128)(2,1)}, u32[]{:S(2)}) copy-start(bf16[64,256]{1,0:T(8,128)(2,1)} %param.25) | copy-start | bytes 98308
  7.2 430.8 %all-gather.3.cloned.1.call-start = ((), (), s32[]{:S(2)}) async-start(), calls=%async_computation | async-start | bytes 8454144 | tf_op jit(solution)/shard_map/all_gather | solution.py:157
  9.1 42.6 %collective-permute-start.1 = (bf16[2,64,8,128]{3,2,1,0:T(8,128)(2,1)S(1)}, bf16[2,64,8,128]{3,2,1,0:T(8,128)(2,1)S(1)}, u32[]{:S(2)}, u32[]{:S(2)}) collective-permute-start(bf16[2,64,8,128]{3,2,1,0:T(8,128)(2,1)S(1)} %bitcast_dynamic-update-slice_fusion), channel_id=1, source_target_pairs={{4,0},{8,4},{12,8},{16,12},{20,16},{24,20},{28,24},{32,28},{36,32}... | collective-permute-start | bytes 786440 | tf_op jit(solution)/shard_map/ppermute | solution.py:21
  17.9 33.9 %collective-permute-start = (bf16[2,64,8,128]{3,2,1,0:T(8,128)(2,1)S(1)}, bf16[2,64,8,128]{3,2,1,0:T(8,128)(2,1)S(1)}, u32[]{:S(2)}, u32[]{:S(2)}) collective-permute-start(bf16[2,64,8,128]{3,2,1,0:T(8,128)(2,1)S(1)} %bitcast_dynamic-update-slice_fusion), channel_id=1, source_target_pairs={{0,4},{4,8},{8,12},{12,16},{16,20},{20,24},{24,28},{28,32},{32,36}... | collective-permute-start | bytes 786440 | tf_op jit(solution)/shard_map/ppermute | solution.py:18
  56.8 3.5 copy-start.4
  57.6 6.4 %copy-start.3 = (bf16[64,1,128]{2,0,1:T(8,128)(2,1)}, bf16[64,1,128]{2,0,1:T(8,128)(2,1)S(1)}, u32[]{:S(2)}) copy-start(bf16[64,1,128]{2,0,1:T(8,128)(2,1)S(1)} %constant_dynamic-slice_fusion.6) | copy-start | bytes 49156 | tf_op jit(solution)/shard_map/while
  78.2 3.5 copy-start.4
  78.9 6.4 %copy-start.3 = (bf16[64,1,128]{2,0,1:T(8,128)(2,1)}, bf16[64,1,128]{2,0,1:T(8,128)(2,1)S(1)}, u32[]{:S(2)}) copy-start(bf16[64,1,128]{2,0,1:T(8,128)(2,1)S(1)} %constant_dynamic-slice_fusion.6) | copy-start | bytes 49156 | tf_op jit(solution)/shard_map/while
  99.5 3.5 copy-start.4
  100.2 6.4 %copy-start.3 = (bf16[64,1,128]{2,0,1:T(8,128)(2,1)}, bf16[64,1,128]{2,0,1:T(8,128)(2,1)S(1)}, u32[]{:S(2)}) copy-start(bf16[64,1,128]{2,0,1:T(8,128)(2,1)S(1)} %constant_dynamic-slice_fusion.6) | copy-start | bytes 49156 | tf_op jit(solution)/shard_map/while
  120.8 3.5 copy-start.4
  121.6 6.4 %copy-start.3 = (bf16[64,1,128]{2,0,1:T(8,128)(2,1)}, bf16[64,1,128]{2,0,1:T(8,128)(2,1)S(1)}, u32[]{:S(2)}) copy-start(bf16[64,1,128]{2,0,1:T(8,128)(2,1)S(1)} %constant_dynamic-slice_fusion.6) | copy-start | bytes 49156 | tf_op jit(solution)/shard_map/while
  142.2 3.5 copy-start.4
  142.9 6.4 %copy-start.3 = (bf16[64,1,128]{2,0,1:T(8,128)(2,1)}, bf16[64,1,128]{2,0,1:T(8,128)(2,1)S(1)}, u32[]{:S(2)}) copy-start(bf16[64,1,128]{2,0,1:T(8,128)(2,1)S(1)} %constant_dynamic-slice_fusion.6) | copy-start | bytes 49156 | tf_op jit(solution)/shard_map/while
  163.5 3.5 copy-start.4
  164.2 6.4 %copy-start.3 = (bf16[64,1,128]{2,0,1:T(8,128)(2,1)}, bf16[64,1,128]{2,0,1:T(8,128)(2,1)S(1)}, u32[]{:S(2)}) copy-start(bf16[64,1,128]{2,0,1:T(8,128)(2,1)S(1)} %constant_dynamic-slice_fusion.6) | copy-start | bytes 49156 | tf_op jit(solution)/shard_map/while
  184.8 3.5 copy-start.4
  185.5 6.4 %copy-start.3 = (bf16[64,1,128]{2,0,1:T(8,128)(2,1)}, bf16[64,1,128]{2,0,1:T(8,128)(2,1)S(1)}, u32[]{:S(2)}) copy-start(bf16[64,1,128]{2,0,1:T(8,128)(2,1)S(1)} %constant_dynamic-slice_fusion.6) | copy-start | bytes 49156 | tf_op jit(solution)/shard_map/while
  206.1 3.5 copy-start.4
  206.8 6.4 %copy-start.3 = (bf16[64,1,128]{2,0,1:T(8,128)(2,1)}, bf16[64,1,128]{2,0,1:T(8,128)(2,1)S(1)}, u32[]{:S(2)}) copy-start(bf16[64,1,128]{2,0,1:T(8,128)(2,1)S(1)} %constant_dynamic-slice_fusion.6) | copy-start | bytes 49156 | tf_op jit(solution)/shard_map/while
  230.0 7.0 %copy-start.2 = (bf16[64,8,128]{2,0,1:T(8,128)(2,1)S(1)}, bf16[64,8,128]{2,0,1:T(8,128)(2,1)}, u32[]{:S(2)}) copy-start(bf16[64,8,128]{2,0,1:T(8,128)(2,1)} %get-tuple-element.290) | copy-start | bytes 393220
  230.1 8.9 %collective-permute-start.3 = (bf16[2,64,8,128]{3,1,2,0:T(8,128)(2,1)S(1)}, bf16[2,64,8,128]{3,1,2,0:T(8,128)(2,1)S(1)}, u32[]{:S(2)}, u32[]{:S(2)}) collective-permute-start(bf16[2,64,8,128]{3,1,2,0:T(8,128)(2,1)S(1)} %pad_maximum_fusion.2), channel_id=1, source_target_pairs={{4,0},{8,4},{12,8},{16,12},{20,16},{24,20},{28,24},{32,28},{36,32}... | collective-permute-start | bytes 786440 | tf_op jit(solution)/shard_map/ppermute | solution.py:29
  234.3 6.0 %collective-permute-start.2 = (bf16[2,64,8,128]{3,1,2,0:T(8,128)(2,1)S(1)}, bf16[2,64,8,128]{3,1,2,0:T(8,128)(2,1)S(1)}, u32[]{:S(2)}, u32[]{:S(2)}) collective-permute-start(bf16[2,64,8,128]{3,1,2,0:T(8,128)(2,1)S(1)} %pad_maximum_fusion.1), channel_id=1, source_target_pairs={{0,4},{4,8},{8,12},{12,16},{16,20},{20,24},{24,28},{28,32},{32,36}... | collective-permute-start | bytes 786440 | tf_op jit(solution)/shard_map/ppermute | solution.py:29
  (1 other events, 1.8 us)
Sparse Core Ops, SparseCore 0:
  228.9 209.0 all-gather.2
